TPU v7x, 256 devices: a whole 4x4x8 slice. The times are simulated.
256 devices in a mesh: sens: 4 (over z_lo, core), par: 64 (over z_hi, x, y).
Axes of the slice: x: 4, y: 4, z: 8 (z_hi: 4, z_lo: 2; z = z_hi * 2 + z_lo), core: 2. Of those that a mesh axis runs over, the one named last changes fastest.
Arguments:
- model: bfloat16 [4, 1024, 256], P('sens', 'par'), may hold values from -6 to 6
- kernel: bfloat16 [512, 1024, 256], P('sens', 'par'), may hold values from -0.01171875 to 0.01171875
- observed: float32 [4, 512, 256], P(None, 'sens'), may hold values from -6 to 6
- weights: float32 [512], P('sens'), may hold values from 0.25 to 4
Outputs:
- gradient: float32 [4, 1024, 256], P('sens', 'par')
- misfit: float32 [], replicated
All inputs are finite; a program needn't handle non-finite values.
Results may differ from a plain program's by a relative error of at most 0.0027.
Values may be sent and summed in bfloat16 or wider, within the bound.
A program may use at most 192 MiB of HBM per device.

v0:
```python
import jax
import jax.numpy as jnp
from jax import lax
from jax.sharding import PartitionSpec as P


def causal_rows(series):
    length_steps = series.shape[-1]
    padded = jnp.concatenate([series, jnp.zeros_like(series)], axis=-1)
    reps = (1,) * (series.ndim - 1) + (length_steps,)
    flat = jnp.tile(padded, reps)
    stride = 2 * length_steps - 1
    flat = flat[..., : length_steps * stride].reshape(series.shape[:-1] + (length_steps, stride))
    return flat[..., :length_steps]


def leading_rows(series):
    length_steps = series.shape[-1]
    padded = jnp.concatenate([series, jnp.zeros_like(series)], axis=-1)
    reps = (1,) * (series.ndim - 1) + (length_steps + 1,)
    flat = jnp.tile(padded, reps)
    stride = 2 * length_steps + 1
    flat = flat[..., : length_steps * stride].reshape(series.shape[:-1] + (length_steps, stride))
    return flat[..., :length_steps]


def local(model, kernel, observed, weights):
    full_model = lax.all_gather(model, "sens", axis=0, tiled=True)
    toeplitz_operator = causal_rows(full_model)
    summed_terms = jnp.einsum(
        "oua,luaz->loz", kernel, toeplitz_operator, preferred_element_type=jnp.float32
    )
    vectors = full_model.shape[0]
    sensors = weights.shape[0]
    steps = full_model.shape[2]
    entries = vectors * sensors * lax.axis_size("sens") * steps
    predicted = lax.psum(summed_terms, "par")
    mismatch = predicted - observed
    weighted_residual = weights[None, :, None] * mismatch
    residual = weighted_residual.astype(jnp.bfloat16)
    squared = lax.psum(jnp.sum(weighted_residual * mismatch), "sens")
    misfit = 0.5 * squared / entries

    def single_adjoint(series):
        shifted = leading_rows(series)
        return jnp.einsum("spk,skt->pt", kernel, shifted, preferred_element_type=jnp.float32)

    adjoint_pieces = lax.map(single_adjoint, residual)
    gradient = lax.psum_scatter(adjoint_pieces, "sens", scatter_dimension=0, tiled=True)
    return (gradient, misfit)


def solution(mesh):
    return jax.shard_map(
        local,
        mesh=mesh,
        in_specs=(P("sens", "par", None), P("sens", "par", None), P(None, "sens", None), P("sens")),
        out_specs=(P("sens", "par", None), P()),
        check_vma=False,
    )
```

profile of v0, /device:TPU:1, one launch (start us, length us, event | category | flops | bytes accessed | tf_op | source)
XLA Modules:
  0.0 1190.9 jit_solution(9768342964295590249)
XLA Ops:
  7.2 0.0 all-reduce.4.cloned.1.call-start
  7.2 8.4 all_gather.3
  15.7 5.9 tile.8
  21.6 17.0 %tile.9 = bf16[4,16,131072]{2,1,0:T(8,128)(2,1)} reshape(bf16[4,16,256,512]{3,2,1,0:T(8,128)(2,1)} %tile.8) | data formatting | bytes 33554432 | tf_op jit(solution)/shard_map/tile | solution.py:11
  38.6 13.7 %slice.16 = bf16[4,16,130816]{2,1,0:T(8,128)(2,1)} slice(bf16[4,16,131072]{2,1,0:T(8,128)(2,1)} %tile.9), slice={[0:4], [0:16], [0:130816]} | slice | bytes 33488896 | tf_op jit(solution)/shard_map/slice | solution.py:13
  52.3 36.2 %reshape.19 = bf16[4,16,256,511]{3,2,1,0:T(8,128)(2,1)} reshape(bf16[4,16,130816]{2,1,0:T(8,128)(2,1)} %slice.16) | data formatting | bytes 33488896 | tf_op jit(solution)/shard_map/reshape | solution.py:13
  88.5 6.6 fusion.10
  95.1 0.0 all-reduce.4.cloned.1.call-update
  95.1 0.0 reduce-scatter.2.cloned.1.call-start
  95.2 1.6 copy.19
  96.8 0.2 copy.18
  97.0 688.3 %all-reduce.4.cloned.1.call-done = f32[4,128,256]{1,2,0:T(8,128)} async-done(((f32[4,128,256]{1,2,0:T(8,128)}), f32[4,128,256]{1,2,0:T(8,128)}) %all-reduce.4.cloned.1.call-update) | async-done | bytes 524304 | tf_op jit(solution)/shard_map/psum | solution.py:37
  785.3 1.9 fusion.15
  787.2 332.0 %while.10 = (s32[]{:T(128)}, f32[4,16,256]{2,1,0:T(8,128)}, bf16[4,128,256]{1,2,0:T(8,128)(2,1)S(1)}, bf16[128,16,256]{0,1,2:T(8,128)(2,1)S(1)}, s32[]{:T(128)}, /*index=5*/bf16[]{:T(256)}) while((s32[]{:T(128)}, f32[4,16,256]{2,1,0:T(8,128)}, bf16[4,128,256]{1,2,0:T(8,128)(2,1)S(1)}, bf16[128,16,256]{0,1,2:T(8,128)(2,1)S(1)}, s32[]{:T(128)}, ...), condition=%wide.region_2.0_spmd, body=%wide.region_1.0_spmd.sunk | while | flops 268435456 | bytes 186466896 | solution.py:48
  787.2 13.5 %tile.21 = bf16[128,257,512]{0,2,1:T(8,128)(2,1)} broadcast(bf16[128,512]{0,1:T(8,128)(2,1)S(1)} %concatenate.8), dimensions={0,2} | broadcast | bytes 33816576 | tf_op jit(solution)/shard_map/while/body/eval_jaxpr/tile | solution.py:21
  800.8 22.9 %slice.31 = bf16[128,131328]{0,1:T(8,128)(2,1)} slice(bf16[128,131584]{0,1:T(8,128)(2,1)} %bitcast.32), slice={[0:128], [0:131328]} | slice | bytes 67239936 | tf_op jit(solution)/shard_map/while/body/eval_jaxpr/slice | solution.py:23
  823.6 37.7 %reshape.24 = bf16[128,256,513]{0,2,1:T(8,128)(2,1)} reshape(bf16[128,131328]{0,1:T(8,128)(2,1)} %slice.31) | data formatting | bytes 67239936 | tf_op jit(solution)/shard_map/while/body/eval_jaxpr/reshape | solution.py:23
  861.3 8.9 fusion.22
  870.2 13.5 %tile.21 = bf16[128,257,512]{0,2,1:T(8,128)(2,1)} broadcast(bf16[128,512]{0,1:T(8,128)(2,1)S(1)} %concatenate.8), dimensions={0,2} | broadcast | bytes 33816576 | tf_op jit(solution)/shard_map/while/body/eval_jaxpr/tile | solution.py:21
  883.7 22.9 %slice.31 = bf16[128,131328]{0,1:T(8,128)(2,1)} slice(bf16[128,131584]{0,1:T(8,128)(2,1)} %bitcast.32), slice={[0:128], [0:131328]} | slice | bytes 67239936 | tf_op jit(solution)/shard_map/while/body/eval_jaxpr/slice | solution.py:23
  906.6 37.7 %reshape.24 = bf16[128,256,513]{0,2,1:T(8,128)(2,1)} reshape(bf16[128,131328]{0,1:T(8,128)(2,1)} %slice.31) | data formatting | bytes 67239936 | tf_op jit(solution)/shard_map/while/body/eval_jaxpr/reshape | solution.py:23
  944.3 8.9 fusion.22
  953.2 13.5 %tile.21 = bf16[128,257,512]{0,2,1:T(8,128)(2,1)} broadcast(bf16[128,512]{0,1:T(8,128)(2,1)S(1)} %concatenate.8), dimensions={0,2} | broadcast | bytes 33816576 | tf_op jit(solution)/shard_map/while/body/eval_jaxpr/tile | solution.py:21
  966.7 22.9 %slice.31 = bf16[128,131328]{0,1:T(8,128)(2,1)} slice(bf16[128,131584]{0,1:T(8,128)(2,1)} %bitcast.32), slice={[0:128], [0:131328]} | slice | bytes 67239936 | tf_op jit(solution)/shard_map/while/body/eval_jaxpr/slice | solution.py:23
  989.6 37.7 %reshape.24 = bf16[128,256,513]{0,2,1:T(8,128)(2,1)} reshape(bf16[128,131328]{0,1:T(8,128)(2,1)} %slice.31) | data formatting | bytes 67239936 | tf_op jit(solution)/shard_map/while/body/eval_jaxpr/reshape | solution.py:23
  1027.2 8.9 fusion.22
  1036.2 13.5 %tile.21 = bf16[128,257,512]{0,2,1:T(8,128)(2,1)} broadcast(bf16[128,512]{0,1:T(8,128)(2,1)S(1)} %concatenate.8), dimensions={0,2} | broadcast | bytes 33816576 | tf_op jit(solution)/shard_map/while/body/eval_jaxpr/tile | solution.py:21
  1049.7 22.9 %slice.31 = bf16[128,131328]{0,1:T(8,128)(2,1)} slice(bf16[128,131584]{0,1:T(8,128)(2,1)} %bitcast.32), slice={[0:128], [0:131328]} | slice | bytes 67239936 | tf_op jit(solution)/shard_map/while/body/eval_jaxpr/slice | solution.py:23
  1072.6 37.7 %reshape.24 = bf16[128,256,513]{0,2,1:T(8,128)(2,1)} reshape(bf16[128,131328]{0,1:T(8,128)(2,1)} %slice.31) | data formatting | bytes 67239936 | tf_op jit(solution)/shard_map/while/body/eval_jaxpr/reshape | solution.py:23
  1110.2 8.9 fusion.22
  1119.2 51.3 %psum.15 = f32[]{:T(128)} all-reduce(f32[]{:T(128)} %get-tuple-element.45), channel_id=1, replica_groups=mesh['sens'=4,'par'=64] {'sens'}, use_global_device_ids=true, to_apply=%region_5.6 | all-reduce | flops 1 | bytes 8 | tf_op jit(solution)/shard_map/psum | solution.py:41
  1171.1 11.8 reduce-scatter.2.cloned.1.call-done
  (17 shorter events, 0.1 us)
Async XLA Ops:
  7.2 778.2 %all-reduce.4.cloned.1.call-start = ((), (), s32[]{:S(2)}) async-start(), calls=%async_computation.1 | async-start | bytes 1048576 | tf_op jit(solution)/shard_map/psum | solution.py:37
  52.3 36.2 %copy-start = (bf16[128,16,256]{2,1,0:T(8,128)(2,1)S(1)}, bf16[128,16,256]{2,1,0:T(8,128)(2,1)}, u32[]{:S(2)}) copy-start(bf16[128,16,256]{2,1,0:T(8,128)(2,1)} %param.7) | copy-start | bytes 3145732
  88.5 8.4 copy-start.1
  88.5 696.9 %copy-start.2 = (f32[128]{0:T(128)S(1)}, f32[128]{0:T(128)}, u32[]{:S(2)}) copy-start(f32[128]{0:T(128)} %param.9) | copy-start | bytes 1540
  95.1 1087.8 %reduce-scatter.2.cloned.1.call-start = ((), (), s32[]{:S(2)}) async-start(), calls=%async_computation.2 | async-start | bytes 81920 | tf_op jit(solution)/shard_map/reduce_scatter | solution.py:49
Sparse Core Ops, SparseCore 0:
  95.2 690.0 all-reduce.3
  1119.3 63.6 reduce-scatter.1
where the time goes:
time: 1200 us; the launch traced here: 1190 us
  waiting for transfers between devices  700 us (58%)
  local copies, waits for them, and re-layouts  371 us (31%)
  blocking collectives  59.7 us (5%)
  matrix products  42.3 us (4%)
  between operations  15.9 us (1%)
    psum x1, waiting for transfers between devices, local(): predicted = lax.psum(summed_terms, 'par')  688 us
    reshape x4, local copies, waits for them, and re-layouts, leading_rows(): flat[..., :length_steps * stride]  151 us
    slice x4, local copies, waits for them, and re-layouts, leading_rows(): flat[..., :length_steps * stride]  91.4 us
    another operation x4, local copies, waits for them, and re-layouts, leading_rows(): flat = jnp.tile(padded, reps)  54.2 us
    psum x1, blocking collectives, local(): squared = lax.psum(jnp.sum(weighted_residual * mismatch), 'sens')  51.3 us
    reshape x1, local copies, waits for them, and re-layouts, causal_rows(): flat[..., :length_steps * stride]  36.2 us
    dot_general x4, matrix products, single_adjoint(): jnp.einsum('spk,skt->pt', kernel, shifted, preferred_element_type=jnp.flo...  35.6 us
  transfers between devices with their start and end apart: 2, of which 2 were waited for; matrix products, arithmetic and copies ran while one was open for 0% of the time, Pallas kernels for 0%

commit v1 on v0

--- a/solution.py
+++ b/solution.py
@@ -34,7 +34,7 @@
     sensors = weights.shape[0]
     steps = full_model.shape[2]
     entries = vectors * sensors * lax.axis_size("sens") * steps
-    predicted = lax.psum(summed_terms, "par")
+    predicted = jnp.sum(lax.all_gather(summed_terms, "par"), axis=0)
     mismatch = predicted - observed
     weighted_residual = weights[None, :, None] * mismatch
     residual = weighted_residual.astype(jnp.bfloat16)

time: 1200 us -> 759 us (0.63)
  waiting for transfers between devices: 700 us -> 297 us
  blocking collectives: 59.7 us -> 16 us
    psum x1 -> x0, waiting for transfers between devices: 688 us -> none  [local(): predicted = lax.psum(summed_terms, 'par')]
    all_gather x0 -> x1, waiting for transfers between devices: none -> 285 us  [local(): predicted = jnp.sum(lax.all_gather(summed_terms, 'par'), axis=0)]
    psum x1, blocking collectives: 51.3 us -> 7.59 us  [local(): squared = lax.psum(jnp.sum(weighted_residual * mismatch), 'sens')]
where the time goes in v1:
time: 759 us; the launch traced here: 755 us
  local copies, waits for them, and re-layouts  372 us (49%)
  waiting for transfers between devices  297 us (39%)
  matrix products  41.4 us (5%)
  blocking collectives  16 us (2%)
  between operations  15.9 us (2%)
  other arithmetic  12.8 us (2%)
    all_gather x1, waiting for transfers between devices, local(): predicted = jnp.sum(lax.all_gather(summed_terms, 'par'), axis=0)  285 us
    reshape x4, local copies, waits for them, and re-layouts, leading_rows(): flat[..., :length_steps * stride]  151 us
    slice x4, local copies, waits for them, and re-layouts, leading_rows(): flat[..., :length_steps * stride]  91.4 us
    another operation x4, local copies, waits for them, and re-layouts, leading_rows(): flat = jnp.tile(padded, reps)  54.2 us
    reshape x1, local copies, waits for them, and re-layouts, causal_rows(): flat[..., :length_steps * stride]  36.2 us
    dot_general x4, matrix products, single_adjoint(): jnp.einsum('spk,skt->pt', kernel, shifted, preferred_element_type=jnp.flo...  35.6 us
    another operation x2, local copies, waits for them, and re-layouts, causal_rows(): flat = jnp.tile(padded, reps)  22.9 us
  transfers between devices with their start and end apart: 2, of which 2 were waited for; matrix products, arithmetic and copies ran while one was open for 0% of the time, Pallas kernels for 0%

profile of v1, /device:TPU:1, one launch (start us, length us, event | category | flops | bytes accessed | tf_op | source)
XLA Modules:
  0.0 755.1 jit_solution(12834045957249988192)
XLA Ops:
  7.2 8.4 %all_gather.9 = bf16[4,16,256]{2,1,0:T(8,128)(2,1)S(1)} all-gather(bf16[1,16,256]{2,1,0:T(8,128)(2,1)} %param.6), channel_id=1, replica_groups=mesh['sens'=4,'par'=64] {'sens'}, dimensions={0}, use_global_device_ids=true | all-gather | bytes 40960 | tf_op jit(solution)/shard_map/all_gather | solution.py:28
  15.7 5.9 tile.8
  21.6 17.0 %tile.9 = bf16[4,16,131072]{2,1,0:T(8,128)(2,1)} reshape(bf16[4,16,256,512]{3,2,1,0:T(8,128)(2,1)} %tile.8) | data formatting | bytes 33554432 | tf_op jit(solution)/shard_map/tile | solution.py:11
  38.6 13.7 %slice.16 = bf16[4,16,130816]{2,1,0:T(8,128)(2,1)} slice(bf16[4,16,131072]{2,1,0:T(8,128)(2,1)} %tile.9), slice={[0:4], [0:16], [0:130816]} | slice | bytes 33488896 | tf_op jit(solution)/shard_map/slice | solution.py:13
  52.3 36.2 %reshape.19 = bf16[4,16,256,511]{3,2,1,0:T(8,128)(2,1)} reshape(bf16[4,16,130816]{2,1,0:T(8,128)(2,1)} %slice.16) | data formatting | bytes 33488896 | tf_op jit(solution)/shard_map/reshape | solution.py:13
  88.5 5.8 fusion.10
  94.2 1.0 copy.22
  95.3 1.6 copy.24
  97.0 284.8 %all-gather.3.cloned.1.call-done = f32[256,128,256]{2,1,0:T(8,128)} async-done(((f32[4,128,256]{2,1,0:T(8,128)}), f32[256,128,256]{2,1,0:T(8,128)}) %all-gather.3.cloned.1.call-update) | async-done | bytes 33554448 | tf_op jit(solution)/shard_map/all_gather | solution.py:37
  381.8 11.9 %reduce_sum.18 = f32[4,128,256]{2,1,0:T(8,128)S(1)} reduce(f32[64,4,128,256]{3,2,1,0:T(8,128)} %bitcast.33, f32[]{:T(128)} %constant.5.clone.1), dimensions={0}, to_apply=%region_0.0 | reduce | flops 8257536 | bytes 34078724 | tf_op jit(solution)/shard_map/reduce_sum | solution.py:37
  393.7 0.9 fusion.15
  394.6 332.5 %while.10 = (s32[]{:T(128)}, f32[4,16,256]{2,1,0:T(8,128)}, bf16[4,128,256]{2,1,0:T(8,128)(2,1)S(1)}, bf16[128,16,256]{0,1,2:T(8,128)(2,1)S(1)}, s32[]{:T(128)}, /*index=5*/bf16[]{:T(256)}) while((s32[]{:T(128)}, f32[4,16,256]{2,1,0:T(8,128)}, bf16[4,128,256]{2,1,0:T(8,128)(2,1)S(1)}, bf16[128,16,256]{0,1,2:T(8,128)(2,1)S(1)}, s32[]{:T(128)}, ...), condition=%wide.region_2.0_spmd, body=%wide.region_1.0_spmd.sunk | while | flops 268435456 | bytes 186597968 | solution.py:48
  394.8 13.5 %tile.21 = bf16[128,257,512]{0,2,1:T(8,128)(2,1)} broadcast(bf16[128,512]{0,1:T(8,128)(2,1)S(1)} %concatenate.8), dimensions={0,2} | broadcast | bytes 33816576 | tf_op jit(solution)/shard_map/while/body/eval_jaxpr/tile | solution.py:21
  408.3 22.9 %slice.31 = bf16[128,131328]{0,1:T(8,128)(2,1)} slice(bf16[128,131584]{0,1:T(8,128)(2,1)} %bitcast.32), slice={[0:128], [0:131328]} | slice | bytes 67239936 | tf_op jit(solution)/shard_map/while/body/eval_jaxpr/slice | solution.py:23
  431.2 37.7 %reshape.25 = bf16[128,256,513]{0,2,1:T(8,128)(2,1)} reshape(bf16[128,131328]{0,1:T(8,128)(2,1)} %slice.31) | data formatting | bytes 67239936 | tf_op jit(solution)/shard_map/while/body/eval_jaxpr/reshape | solution.py:23
  468.8 8.9 %fusion.22 = f32[4,16,256]{2,1,0:T(8,128)} fusion(f32[4,16,256]{2,1,0:T(8,128)} %get-tuple-element.83, s32[]{:T(128)} %get-tuple-element.82, bf16[128,16,256]{0,1,2:T(8,128)(2,1)S(1)} %get-tuple-element.91, bf16[128,256,513]{0,2,1:T(8,128)(2,1)} %reshape.25), kind=kOutput, calls=%fused_computation.3.clone.1 | convolution fusion | flops 268435456 | bytes 17842688 | tf_op jit(solution)/shard_map/while/body/eval_jaxpr/spk,skt->pt/dot_general | solution.py:46
  477.7 0.1 copy.34
  477.9 13.5 %tile.21 = bf16[128,257,512]{0,2,1:T(8,128)(2,1)} broadcast(bf16[128,512]{0,1:T(8,128)(2,1)S(1)} %concatenate.8), dimensions={0,2} | broadcast | bytes 33816576 | tf_op jit(solution)/shard_map/while/body/eval_jaxpr/tile | solution.py:21
  491.4 22.9 %slice.31 = bf16[128,131328]{0,1:T(8,128)(2,1)} slice(bf16[128,131584]{0,1:T(8,128)(2,1)} %bitcast.32), slice={[0:128], [0:131328]} | slice | bytes 67239936 | tf_op jit(solution)/shard_map/while/body/eval_jaxpr/slice | solution.py:23
  514.3 37.7 %reshape.25 = bf16[128,256,513]{0,2,1:T(8,128)(2,1)} reshape(bf16[128,131328]{0,1:T(8,128)(2,1)} %slice.31) | data formatting | bytes 67239936 | tf_op jit(solution)/shard_map/while/body/eval_jaxpr/reshape | solution.py:23
  551.9 8.9 %fusion.22 = f32[4,16,256]{2,1,0:T(8,128)} fusion(f32[4,16,256]{2,1,0:T(8,128)} %get-tuple-element.83, s32[]{:T(128)} %get-tuple-element.82, bf16[128,16,256]{0,1,2:T(8,128)(2,1)S(1)} %get-tuple-element.91, bf16[128,256,513]{0,2,1:T(8,128)(2,1)} %reshape.25), kind=kOutput, calls=%fused_computation.3.clone.1 | convolution fusion | flops 268435456 | bytes 17842688 | tf_op jit(solution)/shard_map/while/body/eval_jaxpr/spk,skt->pt/dot_general | solution.py:46
  560.9 0.1 copy.34
  561.0 13.5 %tile.21 = bf16[128,257,512]{0,2,1:T(8,128)(2,1)} broadcast(bf16[128,512]{0,1:T(8,128)(2,1)S(1)} %concatenate.8), dimensions={0,2} | broadcast | bytes 33816576 | tf_op jit(solution)/shard_map/while/body/eval_jaxpr/tile | solution.py:21
  574.5 22.9 %slice.31 = bf16[128,131328]{0,1:T(8,128)(2,1)} slice(bf16[128,131584]{0,1:T(8,128)(2,1)} %bitcast.32), slice={[0:128], [0:131328]} | slice | bytes 67239936 | tf_op jit(solution)/shard_map/while/body/eval_jaxpr/slice | solution.py:23
  597.4 37.7 %reshape.25 = bf16[128,256,513]{0,2,1:T(8,128)(2,1)} reshape(bf16[128,131328]{0,1:T(8,128)(2,1)} %slice.31) | data formatting | bytes 67239936 | tf_op jit(solution)/shard_map/while/body/eval_jaxpr/reshape | solution.py:23
  635.1 8.9 %fusion.22 = f32[4,16,256]{2,1,0:T(8,128)} fusion(f32[4,16,256]{2,1,0:T(8,128)} %get-tuple-element.83, s32[]{:T(128)} %get-tuple-element.82, bf16[128,16,256]{0,1,2:T(8,128)(2,1)S(1)} %get-tuple-element.91, bf16[128,256,513]{0,2,1:T(8,128)(2,1)} %reshape.25), kind=kOutput, calls=%fused_computation.3.clone.1 | convolution fusion | flops 268435456 | bytes 17842688 | tf_op jit(solution)/shard_map/while/body/eval_jaxpr/spk,skt->pt/dot_general | solution.py:46
  644.1 13.5 %tile.21 = bf16[128,257,512]{0,2,1:T(8,128)(2,1)} broadcast(bf16[128,512]{0,1:T(8,128)(2,1)S(1)} %concatenate.8), dimensions={0,2} | broadcast | bytes 33816576 | tf_op jit(solution)/shard_map/while/body/eval_jaxpr/tile | solution.py:21
  657.7 22.9 %slice.31 = bf16[128,131328]{0,1:T(8,128)(2,1)} slice(bf16[128,131584]{0,1:T(8,128)(2,1)} %bitcast.32), slice={[0:128], [0:131328]} | slice | bytes 67239936 | tf_op jit(solution)/shard_map/while/body/eval_jaxpr/slice | solution.py:23
  680.5 37.7 %reshape.25 = bf16[128,256,513]{0,2,1:T(8,128)(2,1)} reshape(bf16[128,131328]{0,1:T(8,128)(2,1)} %slice.31) | data formatting | bytes 67239936 | tf_op jit(solution)/shard_map/while/body/eval_jaxpr/reshape | solution.py:23
  718.2 8.9 %fusion.22 = f32[4,16,256]{2,1,0:T(8,128)} fusion(f32[4,16,256]{2,1,0:T(8,128)} %get-tuple-element.83, s32[]{:T(128)} %get-tuple-element.82, bf16[128,16,256]{0,1,2:T(8,128)(2,1)S(1)} %get-tuple-element.91, bf16[128,256,513]{0,2,1:T(8,128)(2,1)} %reshape.25), kind=kOutput, calls=%fused_computation.3.clone.1 | convolution fusion | flops 268435456 | bytes 17842688 | tf_op jit(solution)/shard_map/while/body/eval_jaxpr/spk,skt->pt/dot_general | solution.py:46
  727.1 7.6 %psum.7 = f32[]{:T(128)} all-reduce(f32[]{:T(128)} %get-tuple-element.49), channel_id=1, replica_groups=mesh['sens'=4,'par'=64] {'sens'}, use_global_device_ids=true, to_apply=%region_5.6 | all-reduce | flops 1 | bytes 8 | tf_op jit(solution)/shard_map/psum | solution.py:41
  735.3 11.8 %reduce-scatter.2.cloned.1.call-done = f32[1,16,256]{2,1,0:T(8,128)} async-done(((f32[4,16,256]{2,1,0:T(8,128)}), f32[1,16,256]{2,1,0:T(8,128)}) %reduce-scatter.2.cloned.1.call-update) | async-done | bytes 16400 | tf_op jit(solution)/shard_map/reduce_scatter | solution.py:49
  (22 shorter events, 0.4 us)
Async XLA Ops:
  7.2 374.6 %all-gather.3.cloned.1.call-start = ((), (), s32[]{:S(2)}) async-start(), calls=%async_computation.2 | async-start | bytes 34078720 | tf_op jit(solution)/shard_map/all_gather | solution.py:37
  52.3 36.2 %copy-start = (bf16[128,16,256]{2,1,0:T(8,128)(2,1)S(1)}, bf16[128,16,256]{2,1,0:T(8,128)(2,1)}, u32[]{:S(2)}) copy-start(bf16[128,16,256]{2,1,0:T(8,128)(2,1)} %param.7) | copy-start | bytes 3145732
  95.3 651.9 %reduce-scatter.2.cloned.1.call-start = ((), (), s32[]{:S(2)}) async-start(), calls=%async_computation.1 | async-start | bytes 81920 | tf_op jit(solution)/shard_map/reduce_scatter | solution.py:49
  381.8 11.9 %copy-start.1 = (f32[4,128,256]{2,1,0:T(8,128)S(1)}, f32[4,128,256]{2,1,0:T(8,128)}, u32[]{:S(2)}) copy-start(f32[4,128,256]{2,1,0:T(8,128)} %param.8) | copy-start | bytes 1572868
  381.8 11.9 %copy-start.2 = (f32[128]{0:T(128)S(1)}, f32[128]{0:T(128)}, u32[]{:S(2)}) copy-start(f32[128]{0:T(128)} %param.9) | copy-start | bytes 1540
Sparse Core Ops, SparseCore 0:
  95.4 286.3 all-gather.2
  727.2 19.9 reduce-scatter.1
